TPU v7x, 512 devices: a whole 4x8x8 slice. The times are simulated.
512 devices in a mesh: occ: 128 (over y, z, core), virt: 4 (over x).
Axes of the slice: x: 4, y: 8, z: 8, core: 2. Of those that a mesh axis runs over, the one named last changes fastest.
Arguments:
- factors: bfloat16 [768, 98304], P('virt', 'occ'), may hold values from -1 to 1
- occ_energy: float32 [64], replicated, may hold values from -2 to -0.5
- virt_energy: float32 [768], replicated, may hold values from 0.2 to 3
- pair_table: int32 [256, 2], P('occ'), may hold values from 0 to 63, as said below
- pair_count: int32 [128], P('occ'), may hold values from 0 to 2, as said below
Outputs:
- gamma: float32 [768, 98304], P('virt', 'occ')
Inputs may be any that keep to these rules, and one draw needn't show every extreme that they name: `pair_table`: each row holds two different orbitals. `pair_count`: the counts sum to exactly 128, and some host has exactly 2.
All inputs are finite; a program needn't handle non-finite values.
Results may differ from a plain program's by a relative error of at most 0.0029.
Values may be sent and summed in bfloat16 or wider, within the bound.
A program may use at most 64 MiB of HBM per device.

v0:
```python
import jax
import jax.numpy as jnp
from jax import lax
from jax.sharding import PartitionSpec as P


def laid_out(blocks, dim):
    dims = list(blocks.shape[1:])
    dims[dim] *= blocks.shape[0]
    return jnp.moveaxis(blocks, 0, dim).reshape(dims)


def gather_together(arrays, axis, dims):
    ravelled = jnp.concatenate([a.reshape(-1) for a in arrays])
    lines, at, finished = (lax.all_gather(ravelled, axis), 0, [])
    for a, dim in zip(arrays, dims):
        blocks = lines[:, at : at + a.size].reshape(-1, *a.shape)
        finished.append(laid_out(blocks, dim))
        at += a.size
    return tuple(finished)


def body(factors, occ_energy, virt_energy, pair_table, pair_count):
    tables, counts = gather_together((pair_table, pair_count), "occ", (0, 0))
    hosts_total = lax.axis_size("occ")
    per_host = pair_table.shape[0]
    entries = jnp.arange(hosts_total * per_host, dtype=jnp.int32)
    active = entries % per_host < jnp.repeat(counts, per_host)
    live_total = per_host * hosts_total // 2
    slot_count = -(-live_total // hosts_total)
    ranking = jnp.cumsum(active.astype(jnp.int32)) - 1
    targets = jnp.arange(hosts_total * slot_count, dtype=jnp.int32)
    select = (active[None, :] & (ranking[None, :] == targets[:, None])).astype(jnp.int32)
    plan = jnp.sum(select[:, :, None] * tables[None, :, :], axis=1).reshape(
        hosts_total, slot_count, 2
    )
    enabled = jnp.max(select, axis=1).reshape(hosts_total, slot_count)
    column = lax.axis_index("virt")
    myself = lax.axis_index("occ")
    orbital_count = occ_energy.shape[0]
    slab_width = factors.shape[0]
    aux_local = factors.shape[1] // orbital_count
    slab_energy = lax.dynamic_slice_in_dim(virt_energy, column * slab_width, slab_width)
    source_cube = factors.reshape(factors.shape[0], aux_local, orbital_count)

    def one_slot(position, accumulated):
        orbitals = lax.dynamic_index_in_dim(plan, position, 1, keepdims=False)
        flags = lax.dynamic_index_in_dim(enabled, position, 1, keepdims=False)
        targets_flat = orbitals.T.reshape(-1)
        picked = jnp.take(source_cube, targets_flat, axis=2)
        outgoing = picked.reshape(factors.shape[0], aux_local, 2, hosts_total)
        incoming = lax.all_to_all(outgoing, "occ", split_axis=3, concat_axis=1, tiled=True)
        both = lax.all_gather(incoming, "virt", axis=0, tiled=True)
        left = both[:, :, 0, 0]
        right = both[:, :, 1, 0]
        mine = lax.dynamic_index_in_dim(orbitals, myself, 0, keepdims=False)
        live_here = lax.dynamic_index_in_dim(flags, myself, 0, keepdims=False).astype(jnp.float32)
        left_slab = lax.dynamic_slice_in_dim(left, column * slab_width, slab_width, 0)
        right_slab = lax.dynamic_slice_in_dim(right, column * slab_width, slab_width, 0)
        couple_rows = lax.dot_general(
            left_slab, right, (((1,), (1,)), ((), ())), preferred_element_type=jnp.float32
        )
        couple_cols = lax.dot_general(
            left, right_slab, (((1,), (1,)), ((), ())), preferred_element_type=jnp.float32
        )
        energy_sum = jnp.take(occ_energy, mine[0]) + jnp.take(occ_energy, mine[1])
        ampl_rows = couple_rows / (energy_sum - slab_energy[:, None] - virt_energy[None, :])
        ampl_cols = couple_cols / (energy_sum - virt_energy[:, None] - slab_energy[None, :])
        mixed_rows = ((2.0 * ampl_rows - ampl_cols.T) * live_here).astype(jnp.bfloat16)
        mixed_cols = ((2.0 * ampl_cols - ampl_rows.T) * live_here).astype(jnp.bfloat16)
        toward_first = jnp.dot(mixed_rows, right, preferred_element_type=jnp.float32)
        toward_second = lax.dot_general(
            mixed_cols, left, (((0,), (0,)), ((), ())), preferred_element_type=jnp.float32
        )
        packed = jnp.stack(
            [toward_first.astype(jnp.bfloat16), toward_second.astype(jnp.bfloat16)], axis=2
        )
        packed = packed.reshape(slab_width, hosts_total, aux_local, 2, 1)
        returned = lax.all_to_all(packed, "occ", split_axis=1, concat_axis=4, tiled=True)
        onehot = (
            targets_flat[:, None] == jnp.arange(orbital_count, dtype=jnp.int32)[None, :]
        ).astype(jnp.bfloat16)
        added = jnp.dot(
            returned.reshape(slab_width * aux_local, 2 * hosts_total),
            onehot,
            preferred_element_type=jnp.float32,
        )
        return accumulated + added.reshape(accumulated.shape)

    start = jnp.zeros(factors.shape, jnp.float32)
    return lax.fori_loop(0, slot_count, one_slot, start)


def solution(mesh):
    in_specs = (P("virt", "occ"), P(), P(), P("occ", None), P("occ"))
    out_specs = P("virt", "occ")
    return jax.shard_map(body, mesh=mesh, in_specs=in_specs, out_specs=out_specs, check_vma=False)
```

profile of v0, /device:TPU:1, one launch (start us, length us, event | category | flops | bytes accessed | tf_op | source)
XLA Modules:
  0.0 244.3 jit_solution(16003386581368237176)
XLA Ops:
  6.5 1.1 copy.56
  7.7 0.2 copy.57
  8.5 0.8 reshape.178
  9.3 1.3 dynamic-slice.11
  11.2 0.2 add_dynamic-update-slice_fusion
  11.4 27.8 %all-reduce = s32[640]{0:T(1024)S(1)} all-reduce(s32[640]{0:T(1024)S(1)} %add_dynamic-update-slice_fusion), channel_id=2, replica_groups=mesh['occ'=128,'virt'=4] {'occ'}, use_global_device_ids=true, to_apply=%add | all-reduce | flops 640 | bytes 5120
  39.2 0.2 reshape.254
  39.4 0.2 slice_reduce_fusion
  39.6 0.1 mul.46
  39.7 0.1 copy.55
  39.7 0.1 broadcast_in_dim.47
  39.8 0.1 broadcast_in_dim.48
  39.9 0.2 broadcast_in_dim.49
  40.1 0.3 reduce-window.9
  40.4 0.1 slice.32
  40.5 0.1 slice_reduce_fusion.1
  40.6 0.1 add_bitcast_fusion
  40.8 0.2 reshape.180
  41.0 0.1 multiply_reduce_fusion
  41.1 0.8 gather_fusion
  41.9 2.8 %copy.69 = bf16[192,12,2,128]{3,2,0,1:T(2,128)(2,1)} copy(bf16[192,12,2,128]{0,1,3,2:T(8,128)(2,1)S(1)} %bitcast.73) | data formatting | bytes 2359296 | tf_op jit(solution)/shard_map/while/body/eval_jaxpr/jit(_take)/gather | solution.py:50
  44.7 2.3 broadcast_select_fusion
  47.0 3.2 %copy.59 = bf16[192,12,2,128]{0,2,1,3:T(2,128)(2,1)S(1)} copy(bf16[192,12,2,128]{3,2,0,1:T(2,128)(2,1)S(1)} %broadcast_select_fusion) | data formatting | bytes 2359296 | tf_op jit(solution)/shard_map/while/body/eval_jaxpr/jit(_take)/select_n | solution.py:50
  50.2 52.1 %all_to_all.41 = bf16[192,12,2,128]{0,2,1,3:T(2,128)(2,1)S(1)} all-to-all(bf16[192,12,2,128]{0,2,1,3:T(2,128)(2,1)S(1)} %copy.59), channel_id=1, replica_groups=mesh['occ'=128,'virt'=4] {'occ'}, dimensions={3} | all-to-all | bytes 2359296 | tf_op jit(solution)/shard_map/while/body/eval_jaxpr/all_to_all | solution.py:52
  102.3 4.4 %copy.60 = bf16[192,1536,2,1]{1,2,3,0:T(2,128)(2,1)} copy(bf16[192,1536,2,1]{0,2,1,3:T(2,128)(2,1)S(1)} %bitcast.74) | data formatting | bytes 2359296 | tf_op jit(solution)/shard_map/while/body/eval_jaxpr/all_to_all | solution.py:52
  106.8 0.6 fusion.44
  111.5 0.1 fusion.36
  111.6 0.6 dynamic_slice.37
  112.8 0.6 fusion.45
  114.7 0.1 broadcast_subtract_fusion.1
  114.8 44.5 %all-gather.3.cloned.1.call-done = bf16[768,1536,2,1]{1,2,3,0:T(2,128)(2,1)} async-done(((bf16[192,1536,2,1]{1,2,3,0:T(2,128)(2,1)}), bf16[768,1536,2,1]{1,2,3,0:T(2,128)(2,1)}) %all-gather.3.cloned.1.call-update) | async-done | bytes 4718608 | tf_op jit(solution)/shard_map/while/body/eval_jaxpr/all_gather | solution.py:53
  159.3 9.6 %fusion.43 = (bf16[768,1536,1,1]{1,2,3,0:T(2,128)(2,1)S(1)}, bf16[768,1536,1,1]{1,2,3,0:T(2,128)(2,1)S(1)}) fusion(bf16[768,1536,2,1]{1,2,3,0:T(2,128)(2,1)} %all-gather.3.cloned.1.call-done), kind=kLoop, calls=%fused_computation.67 | loop fusion | bytes 9437184 | tf_op jit(solution)/shard_map/while/body/eval_jaxpr/slice | solution.py:55
  168.9 0.6 copy.70
  169.5 0.6 copy.71
  170.1 0.9 fusion.4
  171.0 0.9 fusion.1
  171.9 0.8 convolution_convert_fusion
  172.7 0.8 convolution_convert_fusion.1
  173.6 0.3 copy.64
  173.8 0.2 stack.13
  174.1 0.3 copy.63
  174.3 0.2 stack.12
  174.6 0.4 pad_maximum_fusion
  175.0 2.4 copy.65
  177.5 55.4 %all_to_all.42 = bf16[192,128,12,2,1]{0,3,4,2,1:T(2,128)(2,1)S(1)} all-to-all(bf16[192,128,12,2,1]{0,3,4,2,1:T(2,128)(2,1)S(1)} %copy.65), channel_id=1, replica_groups=mesh['occ'=128,'virt'=4] {'occ'}, dimensions={1} | all-to-all | bytes 2359296 | tf_op jit(solution)/shard_map/while/body/eval_jaxpr/all_to_all | solution.py:79
  232.9 2.9 %copy.66 = bf16[192,1,12,2,128,1]{4,3,2,0,5,1:T(2,128)(2,1)S(1)} copy(bf16[192,1,12,2,128,1]{0,3,2,4,5,1:T(2,128)(2,1)S(1)} %bitcast.75) | data formatting | bytes 2359296 | tf_op jit(solution)/shard_map/while/body/eval_jaxpr/all_to_all | solution.py:79
  235.8 0.5 fusion.6
  236.3 1.1 reshape.186
  (17 shorter events, 0.3 us)
Async XLA Ops:
  6.5 152.7 %all-gather.3.cloned.1.call-start = ((), (), s32[]{:S(2)}) async-start(), calls=%async_computation.2 | async-start | bytes 5898240 | tf_op jit(solution)/shard_map/while/body/eval_jaxpr/all_gather | solution.py:53
  102.3 10.5 %copy-start.1 = (f32[64]{0:T(128)S(1)}, f32[64]{0:T(128)}, u32[]{:S(2)}) copy-start(f32[64]{0:T(128)} %param.6) | copy-start | bytes 772
  102.3 12.3 %copy-start = (f32[768]{0:T(1024)S(1)}, f32[768]{0:T(1024)}, u32[]{:S(2)}) copy-start(f32[768]{0:T(1024)} %param.7) | copy-start | bytes 9220
Sparse Core Ops, SparseCore 0:
  106.9 52.3 all-gather.2
where the time goes:
time: 245 us; the launch traced here: 244 us
  blocking collectives  135 us (55%)
  waiting for transfers between devices  44.5 us (18%)
  local copies, waits for them, and re-layouts  36 us (15%)
  between operations  20.8 us (8%)
  matrix products  3.96 us (2%)
  other arithmetic  3.7 us (2%)
    all_to_all x1, blocking collectives, one_slot(): lax.all_to_all(packed, 'occ', split_axis=1, concat_axis=4, tiled=True)  55.4 us
    all_to_all x1, blocking collectives, one_slot(): lax.all_to_all(outgoing, 'occ', split_axis=3, concat_axis=1, tiled=True)  52.1 us
    all_gather x1, waiting for transfers between devices, one_slot(): both = lax.all_gather(incoming, 'virt', axis=0, tiled=True)  44.5 us
    unnamed x1, blocking collectives  27.8 us
    slice x1, local copies, waits for them, and re-layouts, one_slot(): right = both[:, :, 1, 0]  9.63 us
  transfers between devices with their start and end apart: 1, of which 1 were waited for; matrix products, arithmetic and copies ran while one was open for 1% of the time, Pallas kernels for 0%

commit v1 on v0

v1 whole, which is shorter than its diff:
```python
import functools

import jax
import jax.numpy as jnp
from jax import lax
from jax.experimental import pallas as pl
from jax.experimental.pallas import tpu as pltpu
from jax.sharding import PartitionSpec as P

BF = jnp.bfloat16
F32 = jnp.float32
SIDE = 8
HOSTS = 32
CHUNK = 16


def nt(a, b):
    return lax.dot_general(a, b, (((1,), (1,)), ((), ())), preferred_element_type=F32)


def tn(a, b):
    return lax.dot_general(a, b, (((0,), (0,)), ((), ())), preferred_element_type=F32)


def nn(a, b):
    return jnp.dot(a, b, preferred_element_type=F32)


def swing(t):
    return (2 * (t % 2) - 1) * ((t + 1) // 2)


def column(rows, shape):
    return lax.broadcasted_iota(jnp.int32, shape, rows)


def whole(ref, sem):
    return pltpu.make_async_copy(ref, ref, sem)


def kernel(dims, tab, cnt, occ_ref, virt_ref, f_ref, out_ref, held, table, onehot, picked,
           got, pairs, spread, diff, mixed, back, summed, grams, hop_out, hop_in, last_out, last_in,
           sem_own, xs, xr, ts, tr, fs, fr, bs, br, gs, gr):
    devices, aux, orbitals, slab, virtuals = dims
    me = lax.axis_index("occ")
    plane = lax.axis_index("virt")
    right, left, opposite = (plane + 1) % 4, (plane + 3) % 4, (plane + 2) % 4
    my_y = me // (2 * SIDE)
    my_z = (me // 2) % SIDE
    my_host = my_y * (SIDE // 2) + my_z // 2
    is_host = ((me % 2) + (my_z + my_y) % 2) == 0
    message = 2 * aux
    tiles = message // 8
    rows = HOSTS * message

    barrier = pltpu.get_barrier_semaphore()

    def greet(t, c):
        pl.semaphore_signal(barrier, inc=1, device_id={"occ": (me + t) % devices})
        return c

    pl.semaphore_signal(barrier, inc=1, device_id={"virt": right})
    pl.semaphore_signal(barrier, inc=1, device_id={"virt": left})
    lax.fori_loop(1, devices, greet, 0)
    pl.semaphore_wait(barrier, devices + 1)

    own = pltpu.make_async_copy(f_ref, held.at[plane], sem_own)
    own.start()
    to_right = pltpu.make_async_remote_copy(f_ref, held.at[plane], xs.at[0], xr.at[0], device_id={"virt": right})
    to_left = pltpu.make_async_remote_copy(f_ref, held.at[plane], xs.at[1], xr.at[1], device_id={"virt": left})
    to_right.start()
    to_left.start()

    lane = lax.broadcasted_iota(jnp.int32, (1, 128), 1)
    line = jnp.where(lane == 4, cnt[0], 0)
    for at, (l, s) in enumerate(((0, 0), (0, 1), (1, 0), (1, 1))):
        line = jnp.where(lane == at, tab[l, s] + 1, line)
    table[me] = line

    def tell(t, c):
        pltpu.make_async_remote_copy(
            table.at[me], table.at[me], ts, tr, device_id={"occ": (me + t) % devices}
        ).start()
        return c

    lax.fori_loop(1, devices, tell, 0)
    half = held.shape[1] // 2
    to_right.wait_recv()
    pass_right = pltpu.make_async_remote_copy(
        held.at[left, pl.ds(0, half)], held.at[left, pl.ds(0, half)], xs.at[2], xr.at[2], device_id={"virt": right})
    pass_right.start()
    to_left.wait_recv()
    pass_left = pltpu.make_async_remote_copy(
        held.at[right, pl.ds(half, half)], held.at[right, pl.ds(half, half)], xs.at[3], xr.at[3], device_id={"virt": left})
    pass_left.start()

    whole(table.at[pl.ds(0, devices - 1)], tr).wait()
    listed = table[...].reshape(devices, 128).astype(F32)
    listed_b = listed.astype(BF)
    flipped = listed.T
    count_row = flipped[4:5, :]
    before = (column(0, (128, 128)) < column(1, (128, 128))).astype(F32).astype(BF)
    rank_row = nn(jnp.broadcast_to(count_row, (16, 128)).astype(BF), before)[0:1, :]

    row = column(0, (rows, 1))
    of_host = (row * 2731) // 65536
    inside = row - of_host * message
    second = inside >= aux
    aux_of = jnp.where(second, inside - aux, inside)
    wanted = (of_host + plane * HOSTS).astype(F32)
    pick0 = ((rank_row == wanted) & (count_row > 0.5)).astype(F32).astype(BF)
    pick1 = ((rank_row + 1.0 == wanted) & (count_row > 1.5)).astype(F32).astype(BF)
    found0 = nn(pick0, listed_b)
    found1 = nn(pick1, listed_b)
    orbital = jnp.where(second, found0[:, 1:2] + found1[:, 3:4], found0[:, 0:1] + found1[:, 2:3])
    key = jnp.where(orbital > 0.5, (aux_of * orbitals).astype(F32) + orbital - 1.0, -1.0)
    onehot[...] = (column(1, (rows, aux * orbitals)).astype(F32) == key).astype(F32).astype(BF)

    own.wait()
    pass_right.wait_recv()
    pass_left.wait_recv()
    picked[...] = nt(onehot[...], held[...].reshape(virtuals, aux * orbitals)).reshape(picked.shape).astype(BF)

    def send(t, c):
        y = (my_y + swing(t // 4) + SIDE) % SIDE
        k = y * 4 + (t + my_z) % 4
        dest = (y * SIDE + 2 * (k % 4) + y % 2) * 2
        src = picked.at[pl.ds(k * tiles, tiles)]
        dst = got.at[pl.ds(me * tiles, tiles)]

        @pl.when(dest != me)
        def _():
            pltpu.make_async_remote_copy(src, dst, fs, fr.at[my_y], device_id={"occ": dest}).start()

        @pl.when(dest == me)
        def _():
            pltpu.make_async_copy(src, dst, fr.at[my_y]).start()

        return c

    lax.fori_loop(0, HOSTS, send, 0)

    part = CHUNK * aux
    block = CHUNK * tiles

    @pl.when(is_host)
    def _():
        mine_at = (my_host + plane * HOSTS).astype(F32)
        hit0 = jnp.where((rank_row == mine_at) & (count_row > 0.5), 1.0, 0.0)
        hit1 = jnp.where((rank_row + 1.0 == mine_at) & (count_row > 1.5), 1.0, 0.0)
        first_at = jnp.sum(hit0 * flipped[0:1, :] + hit1 * flipped[2:3, :], axis=1, keepdims=True)
        second_at = jnp.sum(hit0 * flipped[1:2, :] + hit1 * flipped[3:4, :], axis=1, keepdims=True)
        names = (lax.broadcasted_iota(jnp.int32, (1, orbitals), 1) + 1).astype(F32)
        energy = jnp.sum(
            jnp.where(names == first_at, occ_ref[...], 0.0), axis=1, keepdims=True
        ) + jnp.sum(jnp.where(names == second_at, occ_ref[...], 0.0), axis=1, keepdims=True)
        virt_row = virt_ref[...]
        virt_col = jnp.broadcast_to(virt_row, (128, virtuals)).T[:, 0:1]
        spread[...] = 1.0 / (energy - virt_col - virt_row)
        diff[...] = jnp.zeros_like(diff)

        r = column(0, (2 * part, 2 * part))
        c = column(1, (2 * part, 2 * part))
        low = r >= part
        q = jnp.where(low, r - part, r)
        n = (q * 5462) // 65536
        place = n * message + (q - n * aux) + jnp.where(low, 0, aux)
        sorter = (place == c).astype(F32).astype(BF)

        def collect(t, carry):
            g = (my_y - swing(t) + SIDE) % SIDE
            spot = got.at[pl.ds(g * block, block)]
            whole(spot, fr.at[g]).wait()
            here = nn(sorter, spot[...].reshape(2 * part, virtuals)).astype(BF)
            pairs[g] = here
            over = jnp.concatenate([here[part:] * 2.0, -here[:part]], axis=0).astype(BF)
            diff[...] += tn(over, here)
            return carry

        lax.fori_loop(0, SIDE, collect, 0)
        mixed[...] = (diff[...] * spread[...]).astype(BF)

        def give(t, carry):
            g = (my_y + swing(t) + SIDE) % SIDE
            block_b = pairs[g]
            toward_first = nt(block_b[:part], mixed[...]).astype(BF)
            toward_second = nn(block_b[part:], mixed[...]).astype(BF)
            both = jnp.concatenate([toward_second, toward_first], axis=0)
            back[pl.ds(g * block, block)] = tn(sorter, both).reshape(block, 8, virtuals).astype(BF)

            def out(u, cc):
                dest = g * CHUNK + (u + me) % CHUNK
                src = back.at[pl.ds(dest * tiles, tiles)]
                dst = summed.at[pl.ds(my_host * tiles, tiles)]

                @pl.when(dest != me)
                def _():
                    pltpu.make_async_remote_copy(src, dst, bs, br, device_id={"occ": dest}).start()

                @pl.when(dest == me)
                def _():
                    pltpu.make_async_copy(src, dst, br).start()

                return cc

            lax.fori_loop(0, CHUNK, out, 0)
            return carry

        lax.fori_loop(0, SIDE, give, 0)

    whole(summed, br).wait()
    grams[...] = tn(summed[...].reshape(rows, virtuals), onehot[...]).reshape(grams.shape)

    cut = slab // 2
    hop_out[...] = grams[opposite].astype(BF)
    hop_right = pltpu.make_async_remote_copy(
        hop_out.at[pl.ds(0, cut)], hop_in.at[pl.ds(0, cut)], gs.at[0], gr.at[0], device_id={"virt": right})
    hop_left = pltpu.make_async_remote_copy(
        hop_out.at[pl.ds(cut, cut)], hop_in.at[pl.ds(cut, cut)], gs.at[1], gr.at[1], device_id={"virt": left})
    hop_right.start()
    hop_left.start()
    hop_right.wait_recv()
    last_out[0, pl.ds(0, cut)] = (grams[right, pl.ds(0, cut)] + hop_in[pl.ds(0, cut)].astype(F32)).astype(BF)
    last_out[0, pl.ds(cut, cut)] = grams[right, pl.ds(cut, cut)].astype(BF)
    end_right = pltpu.make_async_remote_copy(
        last_out.at[0], last_in.at[0], gs.at[2], gr.at[2], device_id={"virt": right})
    end_right.start()
    hop_left.wait_recv()
    last_out[1, pl.ds(0, cut)] = grams[left, pl.ds(0, cut)].astype(BF)
    last_out[1, pl.ds(cut, cut)] = (grams[left, pl.ds(cut, cut)] + hop_in[pl.ds(cut, cut)].astype(F32)).astype(BF)
    end_left = pltpu.make_async_remote_copy(
        last_out.at[1], last_in.at[1], gs.at[3], gr.at[3], device_id={"virt": left})
    end_left.start()

    to_right.wait_send()
    to_left.wait_send()
    pass_right.wait_send()
    pass_left.wait_send()
    whole(table.at[pl.ds(0, devices - 1)], ts).wait()

    @pl.when(is_host)
    def _():
        whole(picked.at[pl.ds(0, (HOSTS - 1) * tiles)], fs).wait()
        whole(back.at[pl.ds(0, (devices - 1) * tiles)], bs).wait()

    @pl.when(jnp.logical_not(is_host))
    def _():
        whole(picked, fs).wait()

    end_right.wait_recv()
    end_left.wait_recv()
    out_ref[...] = grams[plane] + last_in[0].astype(F32) + last_in[1].astype(F32)
    hop_right.wait_send()
    hop_left.wait_send()
    end_right.wait_send()
    end_left.wait_send()


def body(factors, occ_energy, virt_energy, pair_table, pair_count):
    devices = lax.axis_size("occ")
    orbitals = occ_energy.shape[0]
    virtuals = virt_energy.shape[0]
    slab, width = factors.shape
    aux = width // orbitals
    message = 2 * aux
    tiles = message // 8
    rows = HOSTS * message
    part = CHUNK * aux
    dims = (devices, aux, orbitals, slab, virtuals)
    dma = pltpu.SemaphoreType.DMA
    vmem = pl.BlockSpec(memory_space=pltpu.VMEM)
    smem = pl.BlockSpec(memory_space=pltpu.SMEM)
    return pl.pallas_call(
        functools.partial(kernel, dims),
        out_shape=jax.ShapeDtypeStruct((slab, width), F32),
        in_specs=[smem, smem, vmem, vmem, pl.BlockSpec(memory_space=pl.ANY)],
        out_specs=vmem,
        scratch_shapes=[
            pltpu.VMEM((4, slab // 8, 8, width), BF),
            pltpu.VMEM((devices, 1, 128), jnp.int32),
            pltpu.VMEM((rows, width), BF),
            pltpu.VMEM((HOSTS * tiles, 8, virtuals), BF),
            pltpu.VMEM((devices * tiles, 8, virtuals), BF),
            pltpu.VMEM((SIDE, 2 * part, virtuals), BF),
            pltpu.VMEM((virtuals, virtuals), F32),
            pltpu.VMEM((virtuals, virtuals), F32),
            pltpu.VMEM((virtuals, virtuals), BF),
            pltpu.VMEM((devices * tiles, 8, virtuals), BF),
            pltpu.VMEM((HOSTS * tiles, 8, virtuals), BF),
            pltpu.VMEM((4, slab, width), F32),
            pltpu.VMEM((slab, width), BF),
            pltpu.VMEM((slab, width), BF),
            pltpu.VMEM((2, slab, width), BF),
            pltpu.VMEM((2, slab, width), BF),
            dma(()), dma((4,)), dma((4,)), dma(()), dma(()), dma(()), dma((SIDE,)), dma(()), dma(()),
            dma((4,)), dma((4,)),
        ],
        compiler_params=pltpu.CompilerParams(
            collective_id=0, has_side_effects=True, vmem_limit_bytes=60 * 1024 * 1024
        ),
    )(pair_table, pair_count, occ_energy.reshape(1, -1), virt_energy.reshape(1, -1),
      factors.reshape(slab // 8, 8, width))


def solution(mesh):
    in_specs = (P("virt", "occ"), P(), P(), P("occ", None), P("occ"))
    out_specs = P("virt", "occ")
    return jax.shard_map(body, mesh=mesh, in_specs=in_specs, out_specs=out_specs, check_vma=False)
```

time: 245 us -> 173 us (0.71)
  the two profiles are of different devices: /device:TPU:1 before, /device:TPU:104 now
where the time goes in v1:
time: 173 us
  Pallas kernels  170 us (98%)
  local copies, waits for them, and re-layouts  2.52 us (1%)
    pallas_call x1, Pallas kernels, body(): pl.pallas_call(functools.partial(kernel, dims), out_shape=jax.ShapeDtypeS...  170 us

profile of v1, /device:TPU:104, one launch (start us, length us, event | category | flops | bytes accessed | tf_op | source)
XLA Modules:
  0.0 172.8 jit_solution(14599254883277101053)
XLA Ops:
  0.0 0.0 copy-start
  0.7 0.0 copy-done
  0.7 0.6 reshape.10.virt_ref
  1.3 169.6 %shard_map.55 = f32[192,768]{1,0:T(8,128)} custom-call(s32[2,2]{1,0:T(2,128)} %tab.1, s32[1]{0:T(128)S(6)} %copy.7.cnt, f32[1,64]{1,0:T(1,128)} %bitcast.3, f32[1,768]{1,0:T(1,128)} %reshape.10.virt_ref, bf16[24,8,768]{2,1,0:T(8,128)(2,1)} %bitcast.2), custom_call_target="tpu_custom_call" | custom-call | tf_op jit(solution)/shard_map/pallas_call | solution.py:273
  170.8 1.9 %copy.8 = f32[192,768]{1,0:T(8,128)} copy(f32[192,768]{1,0:T(8,128)} %shard_map.55) | data formatting | bytes 1179648
Async XLA Ops:
  0.0 0.7 copy-start

commit v2 on v1

v2 whole, which is shorter than its diff:
```python
import functools

import jax
import jax.numpy as jnp
from jax import lax
from jax.experimental import pallas as pl
from jax.experimental.pallas import tpu as pltpu
from jax.sharding import PartitionSpec as P

BF = jnp.bfloat16
F32 = jnp.float32
SIDE = 8
HOSTS = SIDE * SIDE
CHUNK = 2 * SIDE


def nt(a, b):
    return lax.dot_general(a, b, (((1,), (1,)), ((), ())), preferred_element_type=F32)


def tn(a, b):
    return lax.dot_general(a, b, (((0,), (0,)), ((), ())), preferred_element_type=F32)


def nn(a, b):
    return jnp.dot(a, b, preferred_element_type=F32)


def swing(t):
    return (2 * (t % 2) - 1) * ((t + 1) // 2)


def offsets(t):
    return swing(t % SIDE), swing((t // SIDE + t) % SIDE)


def iota(axis, shape):
    return lax.broadcasted_iota(jnp.int32, shape, axis)


def ones_where(mask):
    return jnp.where(mask, 1.0, 0.0).astype(BF)


def whole(ref, sem):
    return pltpu.make_async_copy(ref, ref, sem)


def kernel(dims, tab, cnt, occ_ref, virt_ref, f_ref, out_ref, held, table, onehot, picked, got,
           got_other, pairs, spread, forth, turned, mixed, mixed_turned, back, summed, last_out,
           last_in, sem_own, xs, xr, ts, tr, fs, fr, hs, hr, bs, br, gs, gr):
    devices, aux, orbitals, slab = dims
    me = lax.axis_index("occ")
    plane = lax.axis_index("virt")
    group = plane // 2
    mirror = 3 - plane
    mate = group * 2 + 1 - plane % 2
    part_of = (plane + group) % 2
    my_y = me // (2 * SIDE)
    my_z = (me // 2) % SIDE
    my_core = me % 2
    is_host = my_core == 0
    message = 2 * aux
    tiles = message // 8
    width = aux * orbitals
    wide = 2 * slab
    part = CHUNK * aux
    block = CHUNK * tiles
    rows = SIDE * message

    barrier = pltpu.get_barrier_semaphore()

    def greet(t, c):
        pl.semaphore_signal(barrier, inc=1, device_id={"occ": (me + t) % devices})
        return c

    pl.semaphore_signal(barrier, inc=1, device_id={"virt": mirror})
    pl.semaphore_signal(barrier, inc=1, device_id={"virt": mate})
    lax.fori_loop(1, devices, greet, 0)
    pl.semaphore_wait(barrier, devices + 1)

    across = pltpu.make_async_remote_copy(f_ref, held.at[group], xs, xr, device_id={"virt": mirror})
    across.start()
    own = pltpu.make_async_copy(f_ref, held.at[group], sem_own)

    lane = iota(1, (1, 128))
    line = jnp.where(lane == 4, cnt[0], 0)
    for at, (l, s) in enumerate(((0, 0), (0, 1), (1, 0), (1, 1))):
        line = jnp.where(lane == at, tab[l, s] + 1, line)
    table[me] = line

    def tell(t, c):
        pltpu.make_async_remote_copy(
            table.at[me], table.at[me], ts, tr, device_id={"occ": (me + t) % devices}
        ).start()
        return c

    lax.fori_loop(1, devices, tell, 0)

    before = ones_where(iota(0, (128, 128)) < iota(1, (128, 128)))
    step = iota(0, (HOSTS, 1))
    fast, slow = step & 7, step >> 3
    diag = (fast + slow) & 7
    ahead_y = (((fast & 1) << 1) - 1) * ((fast + 1) >> 1)
    ahead_z = (((diag & 1) << 1) - 1) * ((diag + 1) >> 1)
    chip = ((my_y + ahead_y + SIDE) & 7) * SIDE + ((my_z + ahead_z + SIDE) & 7)
    wanted = (chip + group * HOSTS).astype(F32)
    row = iota(0, (rows, 1))
    of_host = (row * 2731) >> 16
    inside = row - of_host * message
    second = inside >= aux
    base = (jnp.where(second, inside - aux, inside) * orbitals).astype(F32) - 1.0
    spots = iota(1, (rows, width)).astype(F32)

    whole(table.at[pl.ds(0, devices - 1)], tr).wait()
    listed = table[...].reshape(devices, 128).astype(F32)
    listed_b = listed.astype(BF)
    flipped = listed.T
    count_row = flipped[4:5, :]
    rank_row = nn(jnp.broadcast_to(count_row, (16, 128)).astype(BF), before)[0:1, :]
    found0 = nn(ones_where((rank_row == wanted) & (count_row > 0.5)), listed_b)
    found1 = nn(ones_where((rank_row + 1.0 == wanted) & (count_row > 1.5)), listed_b)
    found = jnp.where(
        lane == 0,
        found0[:, 0:1] + found1[:, 2:3],
        jnp.where(lane == 1, found0[:, 1:2] + found1[:, 3:4], 0.0),
    ).astype(BF)

    own.start()
    own.wait()
    across.wait_recv()

    def select(e, c):
        spread_out = ones_where(of_host + e * SIDE == iota(1, (rows, HOSTS)))
        both = nn(spread_out, found)
        orbital = jnp.where(second, both[:, 1:2], both[:, 0:1])
        key = jnp.where(orbital > 0.5, base + orbital, -1.0)
        chosen = ones_where(spots == key)
        onehot[pl.ds(e * rows, rows)] = chosen
        picked[pl.ds(e * SIDE * tiles, SIDE * tiles)] = (
            nt(chosen, held[...].reshape(wide, width)).reshape(SIDE * tiles, 8, wide).astype(BF)
        )

        def send(u, cc):
            t = e * SIDE + u
            dy, dz = offsets(t)
            dest = (((my_y + dy + SIDE) % SIDE) * SIDE + (my_z + dz + SIDE) % SIDE) * 2
            src = picked.at[pl.ds(t * tiles, tiles)]
            dst = got.at[pl.ds((2 * t + my_core) * tiles, tiles)]

            @pl.when(dest != me)
            def _():
                pltpu.make_async_remote_copy(src, dst, fs, fr.at[e], device_id={"occ": dest}).start()

            @pl.when(dest == me)
            def _():
                pltpu.make_async_copy(src, dst, fr.at[e]).start()

            return cc

        lax.fori_loop(0, SIDE, send, 0)
        return c

    lax.fori_loop(0, SIDE, select, 0)

    def swap(e):
        spot = pl.ds(e * block, block)
        return pltpu.make_async_remote_copy(
            got.at[spot], got_other.at[spot], hs.at[e], hr.at[e], device_id={"virt": mate})

    @pl.when(is_host)
    def _():
        mine_at = (my_y * SIDE + my_z + group * HOSTS).astype(F32)
        hit0 = jnp.where((rank_row == mine_at) & (count_row > 0.5), 1.0, 0.0)
        hit1 = jnp.where((rank_row + 1.0 == mine_at) & (count_row > 1.5), 1.0, 0.0)
        first_at = jnp.sum(hit0 * flipped[0:1, :] + hit1 * flipped[2:3, :], axis=1, keepdims=True)
        second_at = jnp.sum(hit0 * flipped[1:2, :] + hit1 * flipped[3:4, :], axis=1, keepdims=True)
        names = (iota(1, (1, orbitals)) + 1).astype(F32)
        energy = jnp.sum(
            jnp.where(names == first_at, occ_ref[...], 0.0), axis=1, keepdims=True
        ) + jnp.sum(jnp.where(names == second_at, occ_ref[...], 0.0), axis=1, keepdims=True)
        virt_mine = virt_ref[pl.ds(part_of, 1), :]
        virt_other = virt_ref[pl.ds(1 - part_of, 1), :]
        virt_col = jnp.broadcast_to(virt_mine, (128, wide)).T[:, 0:1]
        spread[:, :wide] = 1.0 / (energy - virt_col - virt_mine)
        spread[:, wide:] = 1.0 / (energy - virt_col - virt_other)
        forth[...] = jnp.zeros_like(forth)
        turned[...] = jnp.zeros_like(turned)

        r = iota(0, (2 * part, 2 * part))
        low = r >= part
        q = jnp.where(low, r - part, r)
        n = (q * 5462) >> 16
        place = n * message + (q - n * aux) + jnp.where(low, 0, aux)
        sorter = ones_where(place == iota(1, (2 * part, 2 * part)))

        def collect(t, carry):
            @pl.when(t < SIDE)
            def _():
                whole(got.at[pl.ds(t * block, block)], fr.at[t]).wait()
                swap(t).start()

            @pl.when(t > 0)
            def _():
                g = t - 1
                spot = pl.ds(g * block, block)
                swap(g).wait_recv()
                mine = nn(sorter, got[spot].reshape(2 * part, wide)).astype(BF)
                other = nn(sorter, got_other[spot].reshape(2 * part, wide)).astype(BF)
                pairs[g, :, :wide] = mine
                pairs[g, :, wide:] = other
                full = jnp.concatenate([mine, other], axis=1)
                forth[...] += tn(mine[part:], full[:part])
                turned[...] += tn(mine[:part], full[part:])

            return carry

        lax.fori_loop(0, SIDE + 1, collect, 0)
        mixed[...] = ((2.0 * forth[...] - turned[...]) * spread[...]).astype(BF)
        mixed_turned[...] = ((2.0 * turned[...] - forth[...]) * spread[...]).astype(BF)

        def give(e, carry):
            both = pairs[e]
            toward_first = nt(both[:part], mixed[...]).astype(BF)
            toward_second = nt(both[part:], mixed_turned[...]).astype(BF)
            sent = jnp.concatenate([toward_second, toward_first], axis=0)
            back[pl.ds(e * block, block)] = tn(sorter, sent).reshape(block, 8, wide).astype(BF)

            def out(u, cc):
                t = e * SIDE + u // 2
                core = u % 2
                dy, dz = offsets(t)
                dest = (((my_y - dy + SIDE) % SIDE) * SIDE + (my_z - dz + SIDE) % SIDE) * 2 + core
                src = back.at[pl.ds((2 * t + core) * tiles, tiles)]
                dst = summed.at[pl.ds(t * tiles, tiles)]

                @pl.when(dest != me)
                def _():
                    pltpu.make_async_remote_copy(src, dst, bs, br, device_id={"occ": dest}).start()

                @pl.when(dest == me)
                def _():
                    pltpu.make_async_copy(src, dst, br).start()

                return cc

            lax.fori_loop(0, CHUNK, out, 0)
            return carry

        lax.fori_loop(0, SIDE, give, 0)

    whole(summed, br).wait()
    grams = tn(summed[...].reshape(HOSTS * message, wide), onehot[...])
    low_part, high_part = grams[:slab], grams[slab:]
    leaving = jnp.where(group == 0, high_part, low_part)
    last_out[...] = leaving.astype(BF)
    end = pltpu.make_async_remote_copy(last_out, last_in, gs, gr, device_id={"virt": mirror})
    end.start()
    out_ref[...] = jnp.where(group == 0, low_part, high_part)

    across.wait_send()
    whole(table.at[pl.ds(0, devices - 1)], ts).wait()

    @pl.when(is_host)
    def _():
        whole(picked.at[pl.ds(0, (HOSTS - 1) * tiles)], fs).wait()
        whole(back.at[pl.ds(0, (devices - 1) * tiles)], bs).wait()

        def sent_swap(e, c):
            swap(e).wait_send()
            return c

        lax.fori_loop(0, SIDE, sent_swap, 0)

    @pl.when(jnp.logical_not(is_host))
    def _():
        whole(picked, fs).wait()

    end.wait_recv()
    out_ref[...] += last_in[...].astype(F32)
    end.wait_send()


def body(factors, occ_energy, virt_energy, pair_table, pair_count):
    devices = lax.axis_size("occ")
    orbitals = occ_energy.shape[0]
    virtuals = virt_energy.shape[0]
    slab, width = factors.shape
    aux = width // orbitals
    message = 2 * aux
    tiles = message // 8
    wide = 2 * slab
    part = CHUNK * aux
    dims = (devices, aux, orbitals, slab)
    dma = pltpu.SemaphoreType.DMA
    vmem = pl.BlockSpec(memory_space=pltpu.VMEM)
    smem = pl.BlockSpec(memory_space=pltpu.SMEM)
    v = virt_energy.reshape(4, slab)
    virt_rows = jnp.stack([jnp.concatenate([v[0], v[3]]), jnp.concatenate([v[1], v[2]])])
    return pl.pallas_call(
        functools.partial(kernel, dims),
        out_shape=jax.ShapeDtypeStruct((slab, width), F32),
        in_specs=[smem, smem, vmem, vmem, pl.BlockSpec(memory_space=pl.ANY)],
        out_specs=vmem,
        scratch_shapes=[
            pltpu.VMEM((2, slab // 8, 8, width), BF),
            pltpu.VMEM((devices, 1, 128), jnp.int32),
            pltpu.VMEM((HOSTS * message, width), BF),
            pltpu.VMEM((HOSTS * tiles, 8, wide), BF),
            pltpu.VMEM((devices * tiles, 8, wide), BF),
            pltpu.VMEM((devices * tiles, 8, wide), BF),
            pltpu.VMEM((SIDE, 2 * part, virtuals), BF),
            pltpu.VMEM((wide, virtuals), F32),
            pltpu.VMEM((wide, virtuals), F32),
            pltpu.VMEM((wide, virtuals), F32),
            pltpu.VMEM((wide, virtuals), BF),
            pltpu.VMEM((wide, virtuals), BF),
            pltpu.VMEM((devices * tiles, 8, wide), BF),
            pltpu.VMEM((HOSTS * tiles, 8, wide), BF),
            pltpu.VMEM((slab, width), BF),
            pltpu.VMEM((slab, width), BF),
            dma(()), dma(()), dma(()), dma(()), dma(()), dma(()), dma((SIDE,)), dma((SIDE,)), dma((SIDE,)),
            dma(()), dma(()), dma(()), dma(()),
        ],
        compiler_params=pltpu.CompilerParams(
            collective_id=0, has_side_effects=True, vmem_limit_bytes=60 * 1024 * 1024
        ),
    )(pair_table, pair_count, occ_energy.reshape(1, -1), virt_rows,
      factors.reshape(slab // 8, 8, width))


def solution(mesh):
    in_specs = (P("virt", "occ"), P(), P(), P("occ", None), P("occ"))
    out_specs = P("virt", "occ")
    return jax.shard_map(body, mesh=mesh, in_specs=in_specs, out_specs=out_specs, check_vma=False)
```

time: 173 us -> 119 us (0.69)
  the two profiles are of different devices: /device:TPU:104 before, /device:TPU:1 now
where the time goes in v2:
time: 119 us; the launch traced here: 118 us
  Pallas kernels  115 us (97%)
  local copies, waits for them, and re-layouts  2.09 us (2%)
    pallas_call x1, Pallas kernels, body(): pl.pallas_call(functools.partial(kernel, dims), out_shape=jax.ShapeDtypeS...  115 us

profile of v2, /device:TPU:1, one launch (start us, length us, event | category | flops | bytes accessed | tf_op | source)
XLA Modules:
  0.0 118.4 jit_solution(10622998520874304337)
XLA Ops:
  0.0 0.0 copy-start
  0.7 0.0 copy-done
  0.7 0.1 concatenate.7
  0.8 0.1 fusion
  0.8 0.1 pad_maximum_fusion.1
  0.9 0.6 pad_maximum_fusion.virt_ref
  1.5 115.0 %shard_map.55 = f32[192,768]{1,0:T(8,128)} custom-call(s32[2,2]{1,0:T(2,128)} %tab.1, s32[1]{0:T(128)S(6)} %copy.7.cnt, f32[1,64]{1,0:T(1,128)} %bitcast.3, f32[2,384]{1,0:T(2,128)} %pad_maximum_fusion.virt_ref, bf16[24,8,768]{2,1,0:T(8,128)(2,1)} %bitcast.2), custom_call_target="tpu_custom_call" | custom-call | tf_op jit(solution)/shard_map/pallas_call | solution.py:300
  116.5 1.9 %copy.8 = f32[192,768]{1,0:T(8,128)} copy(f32[192,768]{1,0:T(8,128)} %shard_map.55) | data formatting | bytes 1179648
  (2 shorter events, 0.0 us)
Async XLA Ops:
  0.0 0.7 copy-start

commit v3 on v2

--- a/solution.py
+++ b/solution.py
@@ -46,9 +46,9 @@
     return pltpu.make_async_copy(ref, ref, sem)
 
 
-def kernel(dims, tab, cnt, occ_ref, virt_ref, f_ref, out_ref, held, table, onehot, picked, got,
-           got_other, pairs, spread, forth, turned, mixed, mixed_turned, back, summed, last_out,
-           last_in, sem_own, xs, xr, ts, tr, fs, fr, hs, hr, bs, br, gs, gr):
+def kernel(dims, tab, cnt, occ_ref, virt_ref, f_ref, out_ref, add_ref, held, table, onehot1, onehot2, picked, got,
+           got_other, pairs, spread, forth, turned, mixed, mixed_turned, back, summed1, summed2, out1, out2,
+           in1, in2, sem_own, xs, xr, ts, tr, fs, fr, hs, hr, bs, br, gs, gr, ps, pr, ls, lr):
     devices, aux, orbitals, slab = dims
     me = lax.axis_index("occ")
     plane = lax.axis_index("virt")
@@ -60,6 +60,8 @@
     my_z = (me // 2) % SIDE
     my_core = me % 2
     is_host = my_core == 0
+    lead = me - my_core
+    twin = me + 1 - 2 * my_core
     message = 2 * aux
     tiles = message // 8
     width = aux * orbitals
@@ -76,8 +78,9 @@
 
     pl.semaphore_signal(barrier, inc=1, device_id={"virt": mirror})
     pl.semaphore_signal(barrier, inc=1, device_id={"virt": mate})
+    pl.semaphore_signal(barrier, inc=1, device_id={"occ": twin, "virt": mate})
     lax.fori_loop(1, devices, greet, 0)
-    pl.semaphore_wait(barrier, devices + 1)
+    pl.semaphore_wait(barrier, devices + 2)
 
     across = pltpu.make_async_remote_copy(f_ref, held.at[group], xs, xr, device_id={"virt": mirror})
     across.start()
@@ -108,9 +111,17 @@
     row = iota(0, (rows, 1))
     of_host = (row * 2731) >> 16
     inside = row - of_host * message
-    second = inside >= aux
-    base = (jnp.where(second, inside - aux, inside) * orbitals).astype(F32) - 1.0
+    second = (inside & 1) > 0
+    base = ((inside >> 1) * orbitals).astype(F32) - 1.0
     spots = iota(1, (rows, width)).astype(F32)
+    edge = SIDE * 16
+    late = row >= edge
+    host2 = jnp.where(late, (row - edge) >> 3, row >> 4)
+    inside2 = jnp.where(late, 16 + (row & 7), row & 15)
+    second2 = (inside2 & 1) > 0
+    base2 = ((inside2 >> 1) * orbitals).astype(F32) - 1.0
+    head = 8 * orbitals
+    rest = width - head
 
     whole(table.at[pl.ds(0, devices - 1)], tr).wait()
     listed = table[...].reshape(devices, 128).astype(F32)
@@ -130,13 +141,16 @@
     own.wait()
     across.wait_recv()
 
+    def slot(t, core):
+        return pl.ds(((t // SIDE) * CHUNK + core * SIDE + t % SIDE) * tiles, tiles)
+
     def select(e, c):
-        spread_out = ones_where(of_host + e * SIDE == iota(1, (rows, HOSTS)))
-        both = nn(spread_out, found)
-        orbital = jnp.where(second, both[:, 1:2], both[:, 0:1])
-        key = jnp.where(orbital > 0.5, base + orbital, -1.0)
-        chosen = ones_where(spots == key)
-        onehot[pl.ds(e * rows, rows)] = chosen
+        def keys(host, odd, start):
+            both = nn(ones_where(host + e * SIDE == iota(1, (rows, HOSTS))), found)
+            orbital = jnp.where(odd, both[:, 1:2], both[:, 0:1])
+            return jnp.where(orbital > 0.5, start + orbital, -1.0)
+
+        chosen = ones_where(spots == keys(of_host, second, base))
         picked[pl.ds(e * SIDE * tiles, SIDE * tiles)] = (
             nt(chosen, held[...].reshape(wide, width)).reshape(SIDE * tiles, 8, wide).astype(BF)
         )
@@ -144,29 +158,84 @@
         def send(u, cc):
             t = e * SIDE + u
             dy, dz = offsets(t)
-            dest = (((my_y + dy + SIDE) % SIDE) * SIDE + (my_z + dz + SIDE) % SIDE) * 2
+            dest = (((my_y + dy + SIDE) % SIDE) * SIDE + (my_z + dz + SIDE) % SIDE) * 2 + my_core
             src = picked.at[pl.ds(t * tiles, tiles)]
-            dst = got.at[pl.ds((2 * t + my_core) * tiles, tiles)]
+            dst = got.at[slot(t, my_core)]
 
             @pl.when(dest != me)
             def _():
-                pltpu.make_async_remote_copy(src, dst, fs, fr.at[e], device_id={"occ": dest}).start()
+                pltpu.make_async_remote_copy(src, dst, fs, fr.at[t], device_id={"occ": dest}).start()
 
             @pl.when(dest == me)
             def _():
-                pltpu.make_async_copy(src, dst, fr.at[e]).start()
+                pltpu.make_async_copy(src, dst, fr.at[t]).start()
 
             return cc
 
         lax.fori_loop(0, SIDE, send, 0)
+        key2 = keys(host2, second2, base2)
+        onehot1[pl.ds(e * edge, edge)] = ones_where(spots[:edge, :head] == key2[:edge])
+        onehot2[pl.ds(e * (rows - edge), rows - edge)] = ones_where(spots[:rows - edge, head:] == key2[edge:])
         return c
 
     lax.fori_loop(0, SIDE, select, 0)
 
-    def swap(e):
-        spot = pl.ds(e * block, block)
+    def pass_on(t):
+        spot = slot(t, my_core)
+        whole(got.at[spot], fr.at[t]).wait()
+        pltpu.make_async_remote_copy(
+            got.at[spot], got_other.at[spot], hs, hr.at[t // SIDE], device_id={"occ": lead, "virt": mate}
+        ).start()
+
+    def beside(e):
+        spot = pl.ds((e * CHUNK + SIDE) * tiles, SIDE * tiles)
         return pltpu.make_async_remote_copy(
-            got.at[spot], got_other.at[spot], hs.at[e], hr.at[e], device_id={"virt": mate})
+            back.at[spot], back.at[spot], ps, pr.at[e], device_id={"occ": twin})
+
+    def give_out(e, phase):
+        def out(u, cc):
+            t = e * SIDE + u
+            dy, dz = offsets(t)
+            dest = (((my_y - dy + SIDE) % SIDE) * SIDE + (my_z - dz + SIDE) % SIDE) * 2 + my_core
+            first_tile = ((t // SIDE) * CHUNK + my_core * SIDE + t % SIDE) * tiles
+            if phase == 0:
+                src, dst = back.at[pl.ds(first_tile, 2)], summed1.at[pl.ds(t * 2, 2)]
+            else:
+                src, dst = back.at[pl.ds(first_tile + 2, 1)], summed2.at[pl.ds(t, 1)]
+
+            @pl.when(dest != me)
+            def _():
+                pltpu.make_async_remote_copy(src, dst, bs, br.at[phase], device_id={"occ": dest}).start()
+
+            @pl.when(dest == me)
+            def _():
+                pltpu.make_async_copy(src, dst, br.at[phase]).start()
+
+            return cc
+
+        lax.fori_loop(0, SIDE, out, 0)
+
+    def give_late(e, c):
+        give_out(e, 1)
+        return c
+
+    @pl.when(jnp.logical_not(is_host))
+    def _():
+        def relay(t, c):
+            pass_on(t)
+            spot = slot(t, 1)
+            pltpu.make_async_remote_copy(
+                got.at[spot], got.at[spot], ls, lr.at[t // SIDE], device_id={"occ": lead}).start()
+            return c
+
+        lax.fori_loop(0, HOSTS, relay, 0)
+
+        def relay_out(e, c):
+            beside(e).wait_recv()
+            give_out(e, 0)
+            return c
+
+        lax.fori_loop(0, SIDE, relay_out, 0)
 
     @pl.when(is_host)
     def _():
@@ -191,20 +260,24 @@
         low = r >= part
         q = jnp.where(low, r - part, r)
         n = (q * 5462) >> 16
-        place = n * message + (q - n * aux) + jnp.where(low, 0, aux)
+        place = n * message + 2 * (q - n * aux) + jnp.where(low, 0, 1)
         sorter = ones_where(place == iota(1, (2 * part, 2 * part)))
 
         def collect(t, carry):
             @pl.when(t < SIDE)
             def _():
-                whole(got.at[pl.ds(t * block, block)], fr.at[t]).wait()
-                swap(t).start()
+                def forward(u, cc):
+                    pass_on(t * SIDE + u)
+                    return cc
+
+                lax.fori_loop(0, SIDE, forward, 0)
 
             @pl.when(t > 0)
             def _():
                 g = t - 1
                 spot = pl.ds(g * block, block)
-                swap(g).wait_recv()
+                whole(got.at[pl.ds(0, SIDE * tiles)], lr.at[g]).wait()
+                whole(got_other.at[spot], hr.at[g]).wait()
                 mine = nn(sorter, got[spot].reshape(2 * part, wide)).astype(BF)
                 other = nn(sorter, got_other[spot].reshape(2 * part, wide)).astype(BF)
                 pairs[g, :, :wide] = mine
@@ -226,59 +299,47 @@
             sent = jnp.concatenate([toward_second, toward_first], axis=0)
             back[pl.ds(e * block, block)] = tn(sorter, sent).reshape(block, 8, wide).astype(BF)
 
-            def out(u, cc):
-                t = e * SIDE + u // 2
-                core = u % 2
-                dy, dz = offsets(t)
-                dest = (((my_y - dy + SIDE) % SIDE) * SIDE + (my_z - dz + SIDE) % SIDE) * 2 + core
-                src = back.at[pl.ds((2 * t + core) * tiles, tiles)]
-                dst = summed.at[pl.ds(t * tiles, tiles)]
-
-                @pl.when(dest != me)
-                def _():
-                    pltpu.make_async_remote_copy(src, dst, bs, br, device_id={"occ": dest}).start()
-
-                @pl.when(dest == me)
-                def _():
-                    pltpu.make_async_copy(src, dst, br).start()
-
-                return cc
-
-            lax.fori_loop(0, CHUNK, out, 0)
+            beside(e).start()
+            give_out(e, 0)
             return carry
 
         lax.fori_loop(0, SIDE, give, 0)
 
-    whole(summed, br).wait()
-    grams = tn(summed[...].reshape(HOSTS * message, wide), onehot[...])
-    low_part, high_part = grams[:slab], grams[slab:]
-    leaving = jnp.where(group == 0, high_part, low_part)
-    last_out[...] = leaving.astype(BF)
-    end = pltpu.make_async_remote_copy(last_out, last_in, gs, gr, device_id={"virt": mirror})
-    end.start()
-    out_ref[...] = jnp.where(group == 0, low_part, high_part)
+    lax.fori_loop(0, SIDE, give_late, 0)
+
+    def finish(phase, summed, onehot, leaving, arriving, columns):
+        whole(summed, br.at[phase]).wait()
+        grams = tn(summed[...].reshape(onehot.shape[0], wide), onehot[...])
+        low_part, high_part = grams[:slab], grams[slab:]
+        leaving[...] = jnp.where(group == 0, high_part, low_part).astype(BF)
+        pltpu.make_async_remote_copy(
+            leaving, arriving, gs.at[phase], gr.at[phase], device_id={"virt": mirror}).start()
+        out_ref[:, columns] = jnp.where(group == 0, low_part, high_part)
+
+    finish(0, summed1, onehot1, out1, in1, pl.ds(0, head))
+    finish(1, summed2, onehot2, out2, in2, pl.ds(head, rest))
 
     across.wait_send()
     whole(table.at[pl.ds(0, devices - 1)], ts).wait()
 
+    whole(picked.at[pl.ds(0, (HOSTS - 1) * tiles)], fs).wait()
+    whole(back.at[pl.ds(0, (HOSTS - 1) * tiles)], bs).wait()
+    whole(got.at[pl.ds(0, HOSTS * tiles)], hs).wait()
+
     @pl.when(is_host)
     def _():
-        whole(picked.at[pl.ds(0, (HOSTS - 1) * tiles)], fs).wait()
-        whole(back.at[pl.ds(0, (devices - 1) * tiles)], bs).wait()
-
-        def sent_swap(e, c):
-            swap(e).wait_send()
-            return c
-
-        lax.fori_loop(0, SIDE, sent_swap, 0)
+        whole(back.at[pl.ds(0, HOSTS * tiles)], ps).wait()
 
     @pl.when(jnp.logical_not(is_host))
     def _():
-        whole(picked, fs).wait()
-
-    end.wait_recv()
-    out_ref[...] += last_in[...].astype(F32)
-    end.wait_send()
+        whole(got.at[pl.ds(0, HOSTS * tiles)], ls).wait()
+
+    whole(in1, gr.at[0]).wait()
+    add_ref[:, :head] = in1[...]
+    whole(in2, gr.at[1]).wait()
+    add_ref[:, head:] = in2[...]
+    whole(out1, gs.at[0]).wait()
+    whole(out2, gs.at[1]).wait()
 
 
 def body(factors, occ_energy, virt_energy, pair_table, pair_count):
@@ -297,15 +358,17 @@
     smem = pl.BlockSpec(memory_space=pltpu.SMEM)
     v = virt_energy.reshape(4, slab)
     virt_rows = jnp.stack([jnp.concatenate([v[0], v[3]]), jnp.concatenate([v[1], v[2]])])
-    return pl.pallas_call(
+    head = 8 * orbitals
+    own, other = pl.pallas_call(
         functools.partial(kernel, dims),
-        out_shape=jax.ShapeDtypeStruct((slab, width), F32),
+        out_shape=(jax.ShapeDtypeStruct((slab, width), F32), jax.ShapeDtypeStruct((slab, width), BF)),
         in_specs=[smem, smem, vmem, vmem, pl.BlockSpec(memory_space=pl.ANY)],
-        out_specs=vmem,
+        out_specs=(vmem, vmem),
         scratch_shapes=[
             pltpu.VMEM((2, slab // 8, 8, width), BF),
             pltpu.VMEM((devices, 1, 128), jnp.int32),
-            pltpu.VMEM((HOSTS * message, width), BF),
+            pltpu.VMEM((HOSTS * 16, head), BF),
+            pltpu.VMEM((HOSTS * 8, width - head), BF),
             pltpu.VMEM((HOSTS * tiles, 8, wide), BF),
             pltpu.VMEM((devices * tiles, 8, wide), BF),
             pltpu.VMEM((devices * tiles, 8, wide), BF),
@@ -316,17 +379,21 @@
             pltpu.VMEM((wide, virtuals), BF),
             pltpu.VMEM((wide, virtuals), BF),
             pltpu.VMEM((devices * tiles, 8, wide), BF),
-            pltpu.VMEM((HOSTS * tiles, 8, wide), BF),
-            pltpu.VMEM((slab, width), BF),
-            pltpu.VMEM((slab, width), BF),
-            dma(()), dma(()), dma(()), dma(()), dma(()), dma(()), dma((SIDE,)), dma((SIDE,)), dma((SIDE,)),
-            dma(()), dma(()), dma(()), dma(()),
+            pltpu.VMEM((HOSTS * 2, 8, wide), BF),
+            pltpu.VMEM((HOSTS, 8, wide), BF),
+            pltpu.VMEM((slab, head), BF),
+            pltpu.VMEM((slab, width - head), BF),
+            pltpu.VMEM((slab, head), BF),
+            pltpu.VMEM((slab, width - head), BF),
+            dma(()), dma(()), dma(()), dma(()), dma(()), dma(()), dma((HOSTS,)), dma(()), dma((SIDE,)),
+            dma(()), dma((2,)), dma((2,)), dma((2,)), dma(()), dma((SIDE,)), dma(()), dma((SIDE,)),
         ],
         compiler_params=pltpu.CompilerParams(
             collective_id=0, has_side_effects=True, vmem_limit_bytes=60 * 1024 * 1024
         ),
     )(pair_table, pair_count, occ_energy.reshape(1, -1), virt_rows,
       factors.reshape(slab // 8, 8, width))
+    return own + other.astype(F32)
 
 
 def solution(mesh):

time: 119 us -> 114 us (0.958)
  Pallas kernels: 115 us -> 110 us
  other arithmetic: 0.66 us -> 2.67 us
  local copies, waits for them, and re-layouts: 2.09 us -> 0.18 us
    pallas_call x1, Pallas kernels: 115 us -> 110 us  [body(): pl.pallas_call(functools.partial(kernel, dims), out_shape=(jax.ShapeDtype...]
    add x0 -> x1, other arithmetic: none -> 2 us  [body(): return own + other.astype(F32)]
    unnamed x3 -> x2, local copies, waits for them, and re-layouts: 1.94 us -> 0.02 us
where the time goes in v3:
time: 114 us
  Pallas kernels  110 us (96%)
  other arithmetic  2.67 us (2%)
    pallas_call x1, Pallas kernels, body(): pl.pallas_call(functools.partial(kernel, dims), out_shape=(jax.ShapeDtype...  110 us

profile of v3, /device:TPU:1, one launch (start us, length us, event | category | flops | bytes accessed | tf_op | source)
XLA Modules:
  0.0 113.7 jit_solution(9050165190071373775)
XLA Ops:
  0.0 0.0 copy-start
  0.7 0.0 copy-done
  0.7 0.1 concatenate.7
  0.8 0.1 fusion
  0.8 0.1 pad_maximum_fusion.1
  0.9 0.6 pad_maximum_fusion.virt_ref
  1.5 110.2 %shard_map.55 = (f32[192,768]{1,0:T(8,128)}, bf16[192,768]{1,0:T(8,128)(2,1)}) custom-call(s32[2,2]{1,0:T(2,128)} %tab.1, s32[1]{0:T(128)S(6)} %copy.6.cnt, f32[1,64]{1,0:T(1,128)} %bitcast.3, f32[2,384]{1,0:T(2,128)} %pad_maximum_fusion.virt_ref, bf16[24,8,768]{2,1,0:T(8,128)(2,1)} %bitcast.2), custom_call_target="tpu_custom_call" | custom-call | tf_op jit(solution)/shard_map/pallas_call | solution.py:362
  111.7 2.0 %convert_add_fusion = f32[192,768]{1,0:T(8,128)} fusion(f32[192,768]{1,0:T(8,128)} %get-tuple-element.7, bf16[192,768]{1,0:T(8,128)(2,1)} %get-tuple-element.8), kind=kLoop, calls=%fused_computation | loop fusion | flops 294912 | bytes 1474560 | tf_op jit(solution)/shard_map/add | solution.py:396
  (2 shorter events, 0.0 us)
Async XLA Ops:
  0.0 0.7 copy-start

commit v4 on v3

--- a/solution.py
+++ b/solution.py
@@ -31,7 +31,7 @@
 
 
 def offsets(t):
-    return swing(t % SIDE), swing((t // SIDE + t) % SIDE)
+    return swing(t % SIDE), swing((t // SIDE + 5 * t) % SIDE)
 
 
 def iota(axis, shape):
@@ -60,6 +60,7 @@
     my_z = (me // 2) % SIDE
     my_core = me % 2
     is_host = my_core == 0
+    way = 1 - 2 * my_core
     lead = me - my_core
     twin = me + 1 - 2 * my_core
     message = 2 * aux
@@ -103,10 +104,10 @@
     before = ones_where(iota(0, (128, 128)) < iota(1, (128, 128)))
     step = iota(0, (HOSTS, 1))
     fast, slow = step & 7, step >> 3
-    diag = (fast + slow) & 7
+    diag = (5 * fast + slow) & 7
     ahead_y = (((fast & 1) << 1) - 1) * ((fast + 1) >> 1)
     ahead_z = (((diag & 1) << 1) - 1) * ((diag + 1) >> 1)
-    chip = ((my_y + ahead_y + SIDE) & 7) * SIDE + ((my_z + ahead_z + SIDE) & 7)
+    chip = ((my_y + way * ahead_y + SIDE) & 7) * SIDE + ((my_z + way * ahead_z + SIDE) & 7)
     wanted = (chip + group * HOSTS).astype(F32)
     row = iota(0, (rows, 1))
     of_host = (row * 2731) >> 16
@@ -158,7 +159,7 @@
         def send(u, cc):
             t = e * SIDE + u
             dy, dz = offsets(t)
-            dest = (((my_y + dy + SIDE) % SIDE) * SIDE + (my_z + dz + SIDE) % SIDE) * 2 + my_core
+            dest = (((my_y + way * dy + SIDE) % SIDE) * SIDE + (my_z + way * dz + SIDE) % SIDE) * 2 + my_core
             src = picked.at[pl.ds(t * tiles, tiles)]
             dst = got.at[slot(t, my_core)]
 
@@ -196,7 +197,7 @@
         def out(u, cc):
             t = e * SIDE + u
             dy, dz = offsets(t)
-            dest = (((my_y - dy + SIDE) % SIDE) * SIDE + (my_z - dz + SIDE) % SIDE) * 2 + my_core
+            dest = (((my_y - way * dy + SIDE) % SIDE) * SIDE + (my_z - way * dz + SIDE) % SIDE) * 2 + my_core
             first_tile = ((t // SIDE) * CHUNK + my_core * SIDE + t % SIDE) * tiles
             if phase == 0:
                 src, dst = back.at[pl.ds(first_tile, 2)], summed1.at[pl.ds(t * 2, 2)]

time: 114 us -> 112 us (0.982)
    pallas_call x1, Pallas kernels: 110 us -> 109 us  [body(): pl.pallas_call(functools.partial(kernel, dims), out_shape=(jax.ShapeDtype...]
where the time goes in v4:
time: 112 us
  Pallas kernels  109 us (97%)
  other arithmetic  2.67 us (2%)
    pallas_call x1, Pallas kernels, body(): pl.pallas_call(functools.partial(kernel, dims), out_shape=(jax.ShapeDtype...  109 us

profile of v4, /device:TPU:1, one launch (start us, length us, event | category | flops | bytes accessed | tf_op | source)
XLA Modules:
  0.0 112.2 jit_solution(16592247982365640396)
XLA Ops:
  0.0 0.0 copy-start
  0.7 0.0 copy-done
  0.7 0.1 concatenate.7
  0.8 0.1 fusion
  0.8 0.1 pad_maximum_fusion.1
  0.9 0.6 pad_maximum_fusion.virt_ref
  1.5 108.7 %shard_map.55 = (f32[192,768]{1,0:T(8,128)}, bf16[192,768]{1,0:T(8,128)(2,1)}) custom-call(s32[2,2]{1,0:T(2,128)} %tab.1, s32[1]{0:T(128)S(6)} %copy.6.cnt, f32[1,64]{1,0:T(1,128)} %bitcast.3, f32[2,384]{1,0:T(2,128)} %pad_maximum_fusion.virt_ref, bf16[24,8,768]{2,1,0:T(8,128)(2,1)} %bitcast.2), custom_call_target="tpu_custom_call" | custom-call | tf_op jit(solution)/shard_map/pallas_call | solution.py:363
  110.2 2.0 %convert_add_fusion = f32[192,768]{1,0:T(8,128)} fusion(f32[192,768]{1,0:T(8,128)} %get-tuple-element.7, bf16[192,768]{1,0:T(8,128)(2,1)} %get-tuple-element.8), kind=kLoop, calls=%fused_computation | loop fusion | flops 294912 | bytes 1474560 | tf_op jit(solution)/shard_map/add | solution.py:397
  (2 shorter events, 0.0 us)
Async XLA Ops:
  0.0 0.7 copy-start
